TPU v7x, 32 devices: a whole 2x2x4 slice. The times are simulated.
32 devices in a mesh: mode: 4 (over y, x), tm: 8 (over z, core).
Axes of the slice: x: 2, y: 2, z: 4, core: 2. Of those that a mesh axis runs over, the one named last changes fastest.
Arguments:
- field: float32 [96, 2, 4096], P('mode', None, 'tm'), may hold values from -6 to 6
- modes: float32 [96, 1024], P(None, 'mode'), may hold values from -0.1875 to 0.1875
- betas: float32 [96, 4], P('mode'), may hold values from -4 to 4
Outputs:
- field_out: float32 [96, 2, 4096], P('mode', None, 'tm')
All inputs are finite; a program needn't handle non-finite values.
Results may differ from a plain program's by a relative error of at most 0.0003.
Values sent between devices are 32-bit elements; how exact they have to be, the bound alone decides.
No kernel may reach another device: no remote copies, remote signals or barrier semaphores. Data moves between devices by JAX's collectives and lax.ppermute only.
A program may use at most 64 MiB of HBM per device.

v0:
```python
import math
import jax
import jax.numpy as jnp
import numpy as np
from jax import lax
from jax.sharding import PartitionSpec as P

RAMAN_TAPS = 256
ITERS = 2
RAMAN_SHARE = 0.18
KERR_GAIN = 6.0
PRECISE = lax.Precision.HIGHEST
BOTH = ("mode", "tm")


def exp_table(product, length):
    angle = product % length * (2.0 * math.pi / length)
    return (np.cos(angle), np.sin(angle))


def block_matrix(cosine, sine):
    return np.stack([np.stack([cosine, -sine], 1), np.stack([sine, cosine], 1)], 0)


def raman_matrix(block, halo):
    positions = np.arange(1, RAMAN_TAPS + 1)
    spacing = 256.0 / RAMAN_TAPS
    raw = np.exp(-positions * spacing / 32.0) * np.sin(positions * spacing / 12.2)
    taps = raw / raw.sum()
    lag = np.arange(block)[None, :] + halo * block - np.arange((halo + 1) * block)[:, None]
    return np.where((lag >= 1) & (lag <= RAMAN_TAPS), taps[np.clip(lag, 1, RAMAN_TAPS) - 1], 0.0)


def general(field, modes, betas):
    n_mode, n_tm = (lax.axis_size("mode"), lax.axis_size("tm"))
    t_index = lax.axis_index("tm")
    own_modes, _, samples = field.shape
    n_dev = n_mode * n_tm
    total = samples * n_tm
    block = total // n_dev
    halo = -(-RAMAN_TAPS // block)
    rows = -(-own_modes // n_tm)
    spare = n_tm * rows - own_modes
    f32 = jnp.float32
    dev, pos = (np.arange(n_dev), np.arange(block))
    cos_a, sin_a = exp_table(dev[:, None] * dev[None, :], n_dev)
    cos_t, sin_t = exp_table(dev[:, None] * pos[None, :], total)
    cos_b, sin_b = exp_table(pos[:, None] * pos[None, :], block)
    first = jnp.asarray(block_matrix(cos_a, sin_a), f32)
    first_back = jnp.asarray(block_matrix(cos_a, -sin_a) / total, f32)
    last = jnp.asarray(block_matrix(cos_b, sin_b), f32)
    last_back = jnp.asarray(block_matrix(cos_b, -sin_b), f32)
    twist = (jnp.asarray(cos_t, f32), jnp.asarray(sin_t, f32))
    frequency = dev[:, None] + n_dev * pos[None, :]
    norm_freq = jnp.asarray(
        np.where(frequency < total // 2, frequency, frequency - total) * (2.0 / total), f32
    )
    rates = lax.dynamic_slice_in_dim(jnp.pad(betas, ((0, spare), (0, 0))), t_index * rows, rows, 0)
    rates = rates[:, :, None, None]
    phase = (
        rates[:, 0]
        + rates[:, 1] * norm_freq
        + rates[:, 2] * (norm_freq * norm_freq) / 2.0
        + rates[:, 3] * (norm_freq * norm_freq * norm_freq) / 6.0
    )
    half_turn = (jnp.cos(phase * 0.5), jnp.sin(phase * 0.5))
    full_turn = (jnp.cos(phase), jnp.sin(phase))

    def disperse(blocks, turn):
        x = jnp.einsum("arcb,cadk->drkb", blocks, first, precision=PRECISE)
        x = jnp.stack([x[0] * twist[0] + x[1] * twist[1], x[1] * twist[0] - x[0] * twist[1]], 0)
        x = jnp.einsum("crkb,cbdq->drkq", x, last, precision=PRECISE)
        x = jnp.stack([x[0] * turn[0] - x[1] * turn[1], x[0] * turn[1] + x[1] * turn[0]], 0)
        x = jnp.einsum("crkq,cqdb->drkb", x, last_back, precision=PRECISE)
        x = jnp.stack([x[0] * twist[0] - x[1] * twist[1], x[1] * twist[0] + x[0] * twist[1]], 0)
        return jnp.einsum("crkb,ckda->ardb", x, first_back, precision=PRECISE)

    raman = jnp.asarray(raman_matrix(block, halo), f32)
    all_profiles = lax.all_gather(modes, "mode", axis=1, tiled=True)
    all_modes = n_mode * own_modes

    def nonlinear(blocks):
        windows = jnp.stack([jnp.roll(blocks, halo - h, axis=0) for h in range(halo + 1)], 3)
        windows = lax.all_to_all(windows, BOTH, 0, 0, tiled=True)
        windows = windows.reshape(n_mode, n_tm * rows, 2, (halo + 1) * block)[:, :own_modes]
        windows = windows.reshape(all_modes, 2, (halo + 1) * block)
        grid = jnp.einsum("pg,pct->cgt", all_profiles, windows, precision=PRECISE)
        intensity = grid[0] * grid[0] + grid[1] * grid[1]
        delayed = jnp.dot(intensity, raman, precision=PRECISE)
        own = slice(halo * block, None)
        weight = (1.0 - RAMAN_SHARE) * intensity[:, own] + RAMAN_SHARE * delayed
        response = jnp.einsum(
            "pg,cgt->pct", all_profiles, grid[:, :, own] * weight, precision=PRECISE
        )
        values = jnp.stack(
            [
                windows[:, 0, own] - KERR_GAIN * response[:, 1],
                windows[:, 1, own] + KERR_GAIN * response[:, 0],
            ],
            1,
        )
        values = jnp.pad(
            values.reshape(n_mode, own_modes, 2, block), ((0, 0), (0, spare), (0, 0), (0, 0))
        )
        return lax.all_to_all(values.reshape(n_dev, rows, 2, block), BOTH, 0, 0, tiled=True)

    entry = jnp.pad(field, ((0, spare), (0, 0), (0, 0))).reshape(n_tm, rows, 2, samples)
    entry = lax.all_to_all(entry, "tm", 0, 0, tiled=True)
    per_tm = samples // block
    blocks = (
        entry.reshape(n_tm, rows, 2, per_tm, block)
        .transpose(0, 3, 1, 2, 4)
        .reshape(n_dev, rows, 2, block)
    )
    blocks = disperse(blocks, half_turn)
    for number in range(ITERS):
        blocks = nonlinear(blocks)
        blocks = disperse(blocks, full_turn if number < ITERS - 1 else half_turn)
    leave = (
        blocks.reshape(n_tm, per_tm, rows, 2, block)
        .transpose(0, 2, 3, 1, 4)
        .reshape(n_tm, rows, 2, samples)
    )
    leave = lax.all_to_all(leave, "tm", 0, 0, tiled=True)
    return leave.reshape(n_tm * rows, 2, samples)[:own_modes]


def solution(mesh):
    return jax.shard_map(
        general,
        mesh=mesh,
        in_specs=(P("mode", None, "tm"), P(None, "mode"), P("mode", None)),
        out_specs=P("mode", None, "tm"),
        check_vma=False,
    )
```

profile of v0, /device:TPU:0, one launch (start us, length us, event | category | flops | bytes accessed | tf_op | source)
XLA Modules:
  0.0 92.2 jit_solution(7750674868088641409)
XLA Ops:
  0.0 0.0 copy-start.9
  0.1 6.5 %all-to-all-start = ((f32[8,3,2,512]{3,2,1,0:T(2,128)}), f32[8,3,2,512]{3,2,1,0:T(2,128)S(1)}, u32[]{:S(2)}, u32[]{:S(2)}) async-start(f32[8,3,2,512]{3,2,1,0:T(2,128)} %bitcast.202), calls=%async_computation | async-start | bytes 196608 | tf_op jit(solution)/shard_map/all_to_all | solution.py:108
  6.6 0.1 constant_dynamic-slice_fusion
  6.7 0.1 copy.33
  6.8 0.2 slice_reduce_fusion.3
  7.0 5.9 %all-to-all-done = f32[8,3,2,512]{3,2,1,0:T(2,128)S(1)} async-done(((f32[8,3,2,512]{3,2,1,0:T(2,128)}), f32[8,3,2,512]{3,2,1,0:T(2,128)S(1)}, u32[]{:S(2)}, u32[]{:S(2)}) %all-to-all-start) | async-done | bytes 98336 | tf_op jit(solution)/shard_map/all_to_all | solution.py:108
  13.0 1.1 %convolution_bitcast_fusion.12 = f32[2,3,32,128]{3,2,0,1:T(8,128)S(1)} fusion(f32[2,32,2,32,1]{1,3,0,2,4:T(8,128)} %constant.49, f32[32,3,2,128,1]{3,2,1,0,4:T(2,128)S(1)} %bitcast.194), kind=kOutput, calls=%fused_computation.24 | convolution fusion | flops 18874368 | bytes 212992 | tf_op jit(solution)/shard_map/arcb,cadk->drkb/dot_general | solution.py:70
  14.1 0.8 multiply_add_fusion.9
  14.9 1.2 %convolution_bitcast_fusion.11 = f32[2,3,32,128]{3,2,0,1:T(8,128)S(1)} fusion(f32[2,128,2,128,1]{3,1,0,2,4:T(8,128)} %constant.50, f32[1,3,32,128]{3,2,0,1:T(8,128)S(1)} %get-tuple-element.30, f32[1,3,32,128]{3,2,0,1:T(8,128)S(1)} %get-tuple-element.29), kind=kOutput, calls=%fused_computation.23 | convolution fusion | flops 75522048 | bytes 458752 | tf_op jit(solution)/shard_map/crkb,cbdq->drkq/dot_general | solution.py:72
  16.1 0.3 multiply_subtract_fusion.7
  16.4 0.3 convolution_bitcast_fusion.10
  16.7 0.3 fusion.16
  17.1 0.9 %copy.34 = f32[32,3,2,3,128]{4,2,1,3,0:T(2,128)} copy(f32[32,3,2,3,128]{4,0,2,1,3:T(8,128)S(1)} %pad_maximum_fusion) | data formatting | bytes 589824 | tf_op jit(solution)/shard_map/stack | solution.py:83
  18.1 3.4 %all-to-all-start.1 = ((f32[32,3,2,3,128]{4,2,1,3,0:T(2,128)}), f32[32,3,2,3,128]{4,2,1,3,0:T(2,128)S(1)}, u32[]{:S(2)}, u32[]{:S(2)}) async-start(f32[32,3,2,3,128]{4,2,1,3,0:T(2,128)} %copy.34), calls=%async_computation.1 | async-start | bytes 589824 | tf_op jit(solution)/shard_map/all_to_all | solution.py:84
  21.5 11.2 %all_gather.3 = f32[96,1024]{1,0:T(8,128)S(1)} all-gather(f32[96,256]{1,0:T(8,128)S(1)} %copy-done.11), channel_id=1, replica_groups=mesh['mode'=4,'tm'=8] {'mode'}, dimensions={1}, use_global_device_ids=true | all-gather | bytes 491520 | tf_op jit(solution)/shard_map/all_gather | solution.py:79
  32.8 0.1 all-to-all-done.1
  32.8 0.1 copy.35
  32.9 0.2 reshape_reshape.6
  33.1 2.7 %convolution_bitcast_fusion.1 = f32[2,1024,384]{1,2,0:T(8,128)S(1)} fusion(f32[96,2,384]{2,0,1:T(8,128)S(1)} %reshape_reshape.6, f32[96,1024]{1,0:T(8,128)S(1)} %all_gather.3), kind=kOutput, calls=%fused_computation.1 | convolution fusion | flops 905969664 | bytes 3833856 | tf_op jit(solution)/shard_map/pg,pct->cgt/dot_general | solution.py:87
  35.8 0.4 fusion.3
  36.2 0.5 copy-done.3
  36.7 1.2 %fusion.5 = f32[1024,128]{0,1:T(8,128)S(1)} fusion(f32[1024,384]{0,1:T(8,128)S(1)} %fusion.3, f32[384,128]{1,0:T(8,128)S(1)} %copy-done.3), kind=kOutput, calls=%fused_computation.13 | convolution fusion | flops 604372992 | bytes 2818048 | tf_op jit(solution)/shard_map/dot_general | solution.py:89
  38.0 1.1 %convolution_bitcast_fusion.3 = f32[96,2,128]{2,0,1:T(8,128)S(1)} fusion(f32[2,1024,384]{1,2,0:T(8,128)S(1)} %convolution_bitcast_fusion.1, f32[1024,128]{0,1:T(8,128)S(1)} %fusion.5, f32[96,1024]{1,0:T(8,128)S(1)} %all_gather.3), kind=kOutput, calls=%fused_computation.15 | convolution fusion | flops 302252032 | bytes 2064384 | tf_op jit(solution)/shard_map/pg,cgt->pct/dot_general | solution.py:92
  39.1 0.1 pad_maximum_fusion.3
  39.2 11.7 %all_to_all.30 = f32[32,3,2,128]{3,2,1,0:T(2,128)S(1)} all-to-all(f32[32,3,2,128]{3,2,1,0:T(2,128)S(1)} %pad_maximum_fusion.3), channel_id=1, replica_groups=mesh['mode'=4,'tm'=8] {'mode','tm'}, dimensions={0} | all-to-all | bytes 196608 | tf_op jit(solution)/shard_map/all_to_all | solution.py:105
  50.9 0.3 convolution_bitcast_fusion.9
  51.2 0.3 convolution_bitcast_fusion.8
  51.5 0.3 multiply_subtract_fusion.4
  51.7 0.3 convolution_bitcast_fusion.7
  52.0 0.3 fusion.23
  52.4 0.2 copy.39
  52.7 13.0 %all_to_all.31 = f32[32,3,2,3,128]{4,2,1,3,0:T(2,128)S(1)} all-to-all(f32[32,3,2,3,128]{4,2,1,3,0:T(2,128)S(1)} %copy.39), channel_id=1, replica_groups=mesh['mode'=4,'tm'=8] {'mode','tm'}, dimensions={0} | all-to-all | bytes 589824 | tf_op jit(solution)/shard_map/all_to_all | solution.py:84
  65.7 0.1 copy.40
  65.8 0.2 reshape_reshape.7
  66.0 2.7 %convolution_bitcast_fusion = f32[2,1024,384]{1,2,0:T(8,128)S(1)} fusion(f32[96,2,384]{2,0,1:T(8,128)S(1)} %reshape_reshape.7, f32[96,1024]{1,0:T(8,128)S(1)} %all_gather.3), kind=kOutput, calls=%fused_computation | convolution fusion | flops 905969664 | bytes 3833856 | tf_op jit(solution)/shard_map/pg,pct->cgt/dot_general | solution.py:87
  68.6 0.4 fusion.1
  69.1 1.2 %fusion.4 = f32[1024,128]{0,1:T(8,128)S(1)} fusion(f32[1024,384]{0,1:T(8,128)S(1)} %fusion.1, f32[384,128]{1,0:T(8,128)S(1)} %copy-done.3), kind=kOutput, calls=%fused_computation.11 | convolution fusion | flops 604372992 | bytes 2818048 | tf_op jit(solution)/shard_map/dot_general | solution.py:89
  70.3 1.1 %convolution_bitcast_fusion.2 = f32[96,2,128]{2,0,1:T(8,128)S(1)} fusion(f32[2,1024,384]{1,2,0:T(8,128)S(1)} %convolution_bitcast_fusion, f32[1024,128]{0,1:T(8,128)S(1)} %fusion.4, f32[96,1024]{1,0:T(8,128)S(1)} %all_gather.3), kind=kOutput, calls=%fused_computation.14 | convolution fusion | flops 302252032 | bytes 2064384 | tf_op jit(solution)/shard_map/pg,cgt->pct/dot_general | solution.py:92
  71.4 0.1 pad_maximum_fusion.4
  71.5 9.7 %all_to_all.32 = f32[32,3,2,128]{3,2,1,0:T(2,128)S(1)} all-to-all(f32[32,3,2,128]{3,2,1,0:T(2,128)S(1)} %pad_maximum_fusion.4), channel_id=1, replica_groups=mesh['mode'=4,'tm'=8] {'mode','tm'}, dimensions={0} | all-to-all | bytes 196608 | tf_op jit(solution)/shard_map/all_to_all | solution.py:105
  81.3 0.3 convolution_bitcast_fusion.6
  81.6 0.3 convolution_bitcast_fusion.5
  81.9 0.3 multiply_subtract_fusion.1
  82.1 0.3 convolution_bitcast_fusion.4
  82.4 0.3 fusion.30
  82.8 0.1 copy.44
  82.9 8.7 %all_to_all.33 = f32[8,3,2,512]{3,2,1,0:T(2,128)S(1)} all-to-all(f32[8,3,2,512]{3,2,1,0:T(2,128)S(1)} %copy.44), channel_id=1, replica_groups=mesh['mode'=4,'tm'=8] {'tm'}, dimensions={0} | all-to-all | bytes 196608 | tf_op jit(solution)/shard_map/all_to_all | solution.py:124
  91.6 0.6 copy.86
  (41 shorter events, 0.4 us)
Async XLA Ops:
  0.0 6.6 %copy-start = (f32[24,4]{0,1:T(4,128)S(1)}, f32[24,4]{0,1:T(4,128)}, u32[]{:S(2)}) copy-start(f32[24,4]{0,1:T(4,128)} %param.13) | copy-start | bytes 1156
  0.0 16.7 %copy-start.4 = (f32[32,128]{1,0:T(8,128)S(1)}, f32[32,128]{1,0:T(8,128)}, u32[]{:S(2)}) copy-start(f32[32,128]{1,0:T(8,128)} %constant.44.clone) | copy-start | bytes 49156
  0.0 16.7 %copy-start.5 = (f32[32,128]{1,0:T(8,128)S(1)}, f32[32,128]{1,0:T(8,128)}, u32[]{:S(2)}) copy-start(f32[32,128]{1,0:T(8,128)} %constant.43.clone) | copy-start | bytes 49156
  0.0 16.1 %copy-start.8 = (f32[32,128]{1,0:T(8,128)S(1)}, f32[32,128]{1,0:T(8,128)}, u32[]{:S(2)}) copy-start(f32[32,128]{1,0:T(8,128)} %constant.48) | copy-start | bytes 49156
  0.0 16.1 %copy-start.9 = (f32[32,128]{1,0:T(8,128)S(1)}, f32[32,128]{1,0:T(8,128)}, u32[]{:S(2)}) copy-start(f32[32,128]{1,0:T(8,128)} %constant.47) | copy-start | bytes 49156
  0.0 16.1 %copy-start.10 = (f32[32,128]{1,0:T(8,128)S(1)}, f32[32,128]{1,0:T(8,128)}, u32[]{:S(2)}) copy-start(f32[32,128]{1,0:T(8,128)} %constant.45.clone) | copy-start | bytes 49156
  0.0 16.4 %copy-start.1 = (f32[2,128,2,128,1]{3,1,0,2,4:T(8,128)S(1)}, f32[2,128,2,128,1]{3,1,0,2,4:T(8,128)}, u32[]{:S(2)}) copy-start(f32[2,128,2,128,1]{3,1,0,2,4:T(8,128)} %constant.51) | copy-start | bytes 786436
  0.1 16.7 %copy-start.6 = (f32[2,32,2,32,1]{1,3,0,2,4:T(8,128)S(1)}, f32[2,32,2,32,1]{1,3,0,2,4:T(8,128)}, u32[]{:S(2)}) copy-start(f32[2,32,2,32,1]{1,3,0,2,4:T(8,128)} %constant.52) | copy-start | bytes 49156
  0.1 12.8 %all-to-all-start = ((f32[8,3,2,512]{3,2,1,0:T(2,128)}), f32[8,3,2,512]{3,2,1,0:T(2,128)S(1)}, u32[]{:S(2)}, u32[]{:S(2)}) async-start(f32[8,3,2,512]{3,2,1,0:T(2,128)} %bitcast.202), calls=%async_computation | async-start | bytes 196608 | tf_op jit(solution)/shard_map/all_to_all | solution.py:108
  16.4 5.1 %copy-start.11 = (f32[96,256]{1,0:T(8,128)S(1)}, f32[96,256]{1,0:T(8,128)}, u32[]{:S(2)}) copy-start(f32[96,256]{1,0:T(8,128)} %param.12) | copy-start | bytes 294916
  18.1 14.8 %all-to-all-start.1 = ((f32[32,3,2,3,128]{4,2,1,3,0:T(2,128)}), f32[32,3,2,3,128]{4,2,1,3,0:T(2,128)S(1)}, u32[]{:S(2)}, u32[]{:S(2)}) async-start(f32[32,3,2,3,128]{4,2,1,3,0:T(2,128)} %copy.34), calls=%async_computation.1 | async-start | bytes 589824 | tf_op jit(solution)/shard_map/all_to_all | solution.py:84
  35.8 0.9 %copy-start.3 = (f32[384,128]{1,0:T(8,128)S(1)}, f32[384,128]{1,0:T(8,128)}, u32[]{:S(2)}) copy-start(f32[384,128]{1,0:T(8,128)} %constant.46.clone) | copy-start | bytes 589828
  37.9 12.9 %copy-start.7 = (f32[2,32,2,32,1]{1,3,0,2,4:T(8,128)S(1)}, f32[2,32,2,32,1]{1,3,0,2,4:T(8,128)}, u32[]{:S(2)}) copy-start(f32[2,32,2,32,1]{1,3,0,2,4:T(8,128)} %constant.49) | copy-start | bytes 49156
  37.9 13.2 %copy-start.2 = (f32[2,128,2,128,1]{3,1,0,2,4:T(8,128)S(1)}, f32[2,128,2,128,1]{3,1,0,2,4:T(8,128)}, u32[]{:S(2)}) copy-start(f32[2,128,2,128,1]{3,1,0,2,4:T(8,128)} %constant.50) | copy-start | bytes 786436
where the time goes:
time: 92.8 us; the launch traced here: 92.2 us
  blocking collectives  54.4 us (59%)
  matrix products  15.1 us (16%)
  starting transfers between devices  9.94 us (11%)
  waiting for transfers between devices  6 us (6%)
  local copies, waits for them, and re-layouts  3.45 us (4%)
  other arithmetic  2.89 us (3%)
    all_to_all x2, blocking collectives, nonlinear(): lax.all_to_all(values.reshape(n_dev, rows, 2, block), BOTH, 0, 0, tiled=T...  21.4 us
    all_to_all x1, blocking collectives, nonlinear(): windows = lax.all_to_all(windows, BOTH, 0, 0, tiled=True)  13 us
    all_gather x1, blocking collectives, general(): all_profiles = lax.all_gather(modes, 'mode', axis=1, tiled=True)  11.2 us
    all_to_all x1, blocking collectives, general(): leave = lax.all_to_all(leave, 'tm', 0, 0, tiled=True)  8.7 us
    all_to_all x1, starting transfers between devices, general(): entry = lax.all_to_all(entry, 'tm', 0, 0, tiled=True)  6.51 us
    all_to_all x1, waiting for transfers between devices, general(): entry = lax.all_to_all(entry, 'tm', 0, 0, tiled=True)  5.92 us
    dot_general x2, matrix products, nonlinear(): grid = jnp.einsum('pg,pct->cgt', all_profiles, windows, precision=PRECISE)  5.32 us
    all_to_all x1, starting transfers between devices, nonlinear(): windows = lax.all_to_all(windows, BOTH, 0, 0, tiled=True)  3.43 us
  transfers between devices with their start and end apart: 2, of which 2 were waited for; matrix products, arithmetic and copies ran while one was open for 0% of the time, Pallas kernels for 0%

commit v1 on v0

--- a/solution.py
+++ b/solution.py
@@ -121,7 +121,19 @@
         .transpose(0, 2, 3, 1, 4)
         .reshape(n_tm, rows, 2, samples)
     )
-    leave = lax.all_to_all(leave, "tm", 0, 0, tiled=True)
+    ways, here = (lax.axis_size("tm"), lax.axis_index("tm"))
+    width = leave.shape[0] // ways
+    lengths = list(leave.shape)
+    lengths[0] = width
+    height = lengths[0]
+    lengths[0] = height * ways
+    full = jnp.zeros(lengths, leave.dtype)
+    for mask in range(ways):
+        part = lax.dynamic_slice_in_dim(leave, (here ^ mask) * width, width, axis=0)
+        if mask:
+            part = lax.ppermute(part, "tm", [(d, d ^ mask) for d in range(ways)])
+        full = lax.dynamic_update_slice_in_dim(full, part, (here ^ mask) * height, axis=0)
+    leave = full
     return leave.reshape(n_tm * rows, 2, samples)[:own_modes]
 
 

time: 92.8 us -> 95.9 us (1.033)
  blocking collectives: 54.4 us -> 35.9 us
  starting transfers between devices: 9.94 us -> 20.7 us
  waiting for transfers between devices: 6 us -> 15.9 us
    all_to_all x2 -> x1, blocking collectives: 21.4 us -> 11.7 us  [nonlinear(): lax.all_to_all(values.reshape(n_dev, rows, 2, block), BOTH, 0, 0, tiled=T...]
    all_to_all x1 -> x0, blocking collectives: 8.7 us -> none  [general(): leave = lax.all_to_all(leave, 'tm', 0, 0, tiled=True)]
    ppermute x0 -> x7, starting transfers between devices: none -> 8.18 us  [general(): part = lax.ppermute(part, 'tm', [(d, d ^ mask) for d in range(ways)])]
    all_to_all x0 -> x1, waiting for transfers between devices: none -> 7.71 us  [nonlinear(): lax.all_to_all(values.reshape(n_dev, rows, 2, block), BOTH, 0, 0, tiled=T...]
    all_to_all x0 -> x1, starting transfers between devices: none -> 2.57 us  [nonlinear(): lax.all_to_all(values.reshape(n_dev, rows, 2, block), BOTH, 0, 0, tiled=T...]
    ppermute x0 -> x7, waiting for transfers between devices: none -> 2.18 us  [general(): part = lax.ppermute(part, 'tm', [(d, d ^ mask) for d in range(ways)])]
  transfers between devices with their start and end apart: 2 -> 10, of which waited for: 2 -> 5; matrix products, arithmetic and copies ran while one was open for 0% -> 1% of each run, Pallas kernels for 0% -> 0%
where the time goes in v1:
time: 95.9 us; the launch traced here: 95.3 us
  blocking collectives  35.9 us (37%)
  starting transfers between devices  20.7 us (22%)
  waiting for transfers between devices  15.9 us (17%)
  matrix products  15.1 us (16%)
  local copies, waits for them, and re-layouts  3.63 us (4%)
  other arithmetic  3.53 us (4%)
    all_to_all x1, blocking collectives, nonlinear(): windows = lax.all_to_all(windows, BOTH, 0, 0, tiled=True)  13 us
    all_to_all x1, blocking collectives, nonlinear(): lax.all_to_all(values.reshape(n_dev, rows, 2, block), BOTH, 0, 0, tiled=T...  11.7 us
    all_gather x1, blocking collectives, general(): all_profiles = lax.all_gather(modes, 'mode', axis=1, tiled=True)  11.2 us
    ppermute x7, starting transfers between devices, general(): part = lax.ppermute(part, 'tm', [(d, d ^ mask) for d in range(ways)])  8.18 us
    all_to_all x1, waiting for transfers between devices, nonlinear(): lax.all_to_all(values.reshape(n_dev, rows, 2, block), BOTH, 0, 0, tiled=T...  7.71 us
    all_to_all x1, starting transfers between devices, general(): entry = lax.all_to_all(entry, 'tm', 0, 0, tiled=True)  6.51 us
    all_to_all x1, waiting for transfers between devices, general(): entry = lax.all_to_all(entry, 'tm', 0, 0, tiled=True)  5.92 us
    dot_general x2, matrix products, nonlinear(): grid = jnp.einsum('pg,pct->cgt', all_profiles, windows, precision=PRECISE)  5.33 us
  transfers between devices with their start and end apart: 10, of which 5 were waited for; matrix products, arithmetic and copies ran while one was open for 1% of the time, Pallas kernels for 0%

profile of v1, /device:TPU:0, one launch (start us, length us, event | category | flops | bytes accessed | tf_op | source)
XLA Modules:
  0.0 95.3 jit_solution(14312212069696858587)
XLA Ops:
  0.1 6.5 %all-to-all-start = ((f32[8,3,2,512]{3,2,1,0:T(2,128)}), f32[8,3,2,512]{3,2,1,0:T(2,128)S(1)}, u32[]{:S(2)}, u32[]{:S(2)}) async-start(f32[8,3,2,512]{3,2,1,0:T(2,128)} %bitcast.201), calls=%async_computation | async-start | bytes 196608 | tf_op jit(solution)/shard_map/all_to_all | solution.py:108
  6.8 0.2 slice_reduce_fusion.3
  7.0 5.9 %all-to-all-done = f32[8,3,2,512]{3,2,1,0:T(2,128)S(1)} async-done(((f32[8,3,2,512]{3,2,1,0:T(2,128)}), f32[8,3,2,512]{3,2,1,0:T(2,128)S(1)}, u32[]{:S(2)}, u32[]{:S(2)}) %all-to-all-start) | async-done | bytes 98336 | tf_op jit(solution)/shard_map/all_to_all | solution.py:108
  13.0 1.1 %convolution_bitcast_fusion.12 = f32[2,3,32,128]{3,2,0,1:T(8,128)S(1)} fusion(f32[2,32,2,32,1]{1,3,0,2,4:T(8,128)} %constant.65, f32[32,3,2,128,1]{3,2,1,0,4:T(2,128)S(1)} %bitcast.194), kind=kOutput, calls=%fused_computation.24 | convolution fusion | flops 18874368 | bytes 212992 | tf_op jit(solution)/shard_map/arcb,cadk->drkb/dot_general | solution.py:70
  14.1 0.8 multiply_add_fusion.9
  14.9 1.2 %convolution_bitcast_fusion.11 = f32[2,3,32,128]{3,2,0,1:T(8,128)S(1)} fusion(f32[2,128,2,128,1]{3,1,0,2,4:T(8,128)} %constant.66, f32[1,3,32,128]{3,2,0,1:T(8,128)S(1)} %get-tuple-element.30, f32[1,3,32,128]{3,2,0,1:T(8,128)S(1)} %get-tuple-element.29), kind=kOutput, calls=%fused_computation.23 | convolution fusion | flops 75522048 | bytes 458752 | tf_op jit(solution)/shard_map/crkb,cbdq->drkq/dot_general | solution.py:72
  16.1 0.3 multiply_subtract_fusion.7
  16.4 0.3 convolution_bitcast_fusion.10
  16.8 0.3 fusion.16
  17.1 0.9 copy.48
  18.1 3.4 %all-to-all-start.1 = ((f32[32,3,2,3,128]{4,2,1,3,0:T(2,128)}), f32[32,3,2,3,128]{4,2,1,3,0:T(2,128)S(1)}, u32[]{:S(2)}, u32[]{:S(2)}) async-start(f32[32,3,2,3,128]{4,2,1,3,0:T(2,128)} %copy.48), calls=%async_computation.1 | async-start | bytes 589824 | tf_op jit(solution)/shard_map/all_to_all | solution.py:84
  21.5 11.2 %all_gather.3 = f32[96,1024]{1,0:T(8,128)S(1)} all-gather(f32[96,256]{1,0:T(8,128)S(1)} %copy-done.12), channel_id=1, replica_groups=mesh['mode'=4,'tm'=8] {'mode'}, dimensions={1}, use_global_device_ids=true | all-gather | bytes 491520 | tf_op jit(solution)/shard_map/all_gather | solution.py:79
  32.9 0.2 reshape_reshape.6
  33.1 2.7 %convolution_bitcast_fusion.1 = f32[2,1024,384]{1,2,0:T(8,128)S(1)} fusion(f32[96,2,384]{2,0,1:T(8,128)S(1)} %reshape_reshape.6, f32[96,1024]{1,0:T(8,128)S(1)} %all_gather.3), kind=kOutput, calls=%fused_computation.1 | convolution fusion | flops 905969664 | bytes 3833856 | tf_op jit(solution)/shard_map/pg,pct->cgt/dot_general | solution.py:87
  35.8 0.4 fusion.3
  36.2 0.5 copy-done.3
  36.7 1.2 %fusion.5 = f32[1024,128]{0,1:T(8,128)S(1)} fusion(f32[1024,384]{0,1:T(8,128)S(1)} %fusion.3, f32[384,128]{1,0:T(8,128)S(1)} %copy-done.3), kind=kOutput, calls=%fused_computation.13 | convolution fusion | flops 604372992 | bytes 2818048 | tf_op jit(solution)/shard_map/dot_general | solution.py:89
  38.0 1.1 %convolution_bitcast_fusion.3 = f32[96,2,128]{2,0,1:T(8,128)S(1)} fusion(f32[2,1024,384]{1,2,0:T(8,128)S(1)} %convolution_bitcast_fusion.1, f32[1024,128]{0,1:T(8,128)S(1)} %fusion.5, f32[96,1024]{1,0:T(8,128)S(1)} %all_gather.3), kind=kOutput, calls=%fused_computation.15 | convolution fusion | flops 302252032 | bytes 2064384 | tf_op jit(solution)/shard_map/pg,cgt->pct/dot_general | solution.py:92
  39.2 11.7 %all_to_all.25 = f32[32,3,2,128]{3,2,1,0:T(2,128)S(1)} all-to-all(f32[32,3,2,128]{3,2,1,0:T(2,128)S(1)} %pad_maximum_fusion.3), channel_id=1, replica_groups=mesh['mode'=4,'tm'=8] {'mode','tm'}, dimensions={0} | all-to-all | bytes 196608 | tf_op jit(solution)/shard_map/all_to_all | solution.py:105
  50.9 0.3 convolution_bitcast_fusion.9
  51.2 0.3 convolution_bitcast_fusion.8
  51.5 0.3 multiply_subtract_fusion.4
  51.7 0.3 convolution_bitcast_fusion.7
  52.0 0.3 fusion.23
  52.4 0.2 copy.53
  52.7 13.0 %all_to_all.26 = f32[32,3,2,3,128]{4,2,1,3,0:T(2,128)S(1)} all-to-all(f32[32,3,2,3,128]{4,2,1,3,0:T(2,128)S(1)} %copy.53), channel_id=1, replica_groups=mesh['mode'=4,'tm'=8] {'mode','tm'}, dimensions={0} | all-to-all | bytes 589824 | tf_op jit(solution)/shard_map/all_to_all | solution.py:84
  65.8 0.2 reshape_reshape.7
  66.0 2.7 %convolution_bitcast_fusion = f32[2,1024,384]{1,2,0:T(8,128)S(1)} fusion(f32[96,2,384]{2,0,1:T(8,128)S(1)} %reshape_reshape.7, f32[96,1024]{1,0:T(8,128)S(1)} %all_gather.3), kind=kOutput, calls=%fused_computation | convolution fusion | flops 905969664 | bytes 3833856 | tf_op jit(solution)/shard_map/pg,pct->cgt/dot_general | solution.py:87
  68.6 0.4 fusion.1
  69.1 1.2 %fusion.4 = f32[1024,128]{0,1:T(8,128)S(1)} fusion(f32[1024,384]{0,1:T(8,128)S(1)} %fusion.1, f32[384,128]{1,0:T(8,128)S(1)} %copy-done.3), kind=kOutput, calls=%fused_computation.11 | convolution fusion | flops 604372992 | bytes 2818048 | tf_op jit(solution)/shard_map/dot_general | solution.py:89
  70.3 1.1 %convolution_bitcast_fusion.2 = f32[96,2,128]{2,0,1:T(8,128)S(1)} fusion(f32[2,1024,384]{1,2,0:T(8,128)S(1)} %convolution_bitcast_fusion, f32[1024,128]{0,1:T(8,128)S(1)} %fusion.4, f32[96,1024]{1,0:T(8,128)S(1)} %all_gather.3), kind=kOutput, calls=%fused_computation.14 | convolution fusion | flops 302252032 | bytes 2064384 | tf_op jit(solution)/shard_map/pg,cgt->pct/dot_general | solution.py:92
  71.4 0.7 pad_maximum_fusion.4
  72.2 2.6 %all-to-all-start.4 = ((f32[32,3,2,128]{3,2,1,0:T(2,128)}), f32[32,3,2,128]{3,2,1,0:T(2,128)S(1)}, u32[]{:S(2)}, u32[]{:S(2)}) async-start(f32[32,3,2,128]{3,2,1,0:T(2,128)} %pad_maximum_fusion.4), calls=%async_computation.4 | async-start | bytes 196608 | tf_op jit(solution)/shard_map/all_to_all | solution.py:105
  74.8 7.7 %all-to-all-done.4 = f32[32,3,2,128]{3,2,1,0:T(2,128)S(1)} async-done(((f32[32,3,2,128]{3,2,1,0:T(2,128)}), f32[32,3,2,128]{3,2,1,0:T(2,128)S(1)}, u32[]{:S(2)}, u32[]{:S(2)}) %all-to-all-start.4) | async-done | bytes 98336 | tf_op jit(solution)/shard_map/all_to_all | solution.py:105
  82.5 0.3 convolution_bitcast_fusion.6
  82.8 0.3 convolution_bitcast_fusion.5
  83.1 0.3 multiply_subtract_fusion.1
  83.4 0.3 convolution_bitcast_fusion.4
  83.7 0.3 fusion.30
  84.1 0.2 collective-permute-start
  84.4 0.4 collective-permute-start.1
  84.8 1.3 %collective-permute-start.2 = (f32[1,3,2,512]{3,2,1,0:T(2,128)S(1)}, f32[1,3,2,512]{3,2,1,0:T(2,128)S(1)}, u32[]{:S(2)}, u32[]{:S(2)}) collective-permute-start(f32[1,3,2,512]{3,2,1,0:T(2,128)S(1)} %copy.103), channel_id=1, source_target_pairs={{0,3},{1,2},{2,1},{3,0},{4,7},{5,6},{6,5},{7,4},{8,11},{9,10},{10,... | collective-permute-start | bytes 36872 | tf_op jit(solution)/shard_map/ppermute | solution.py:134
  86.2 2.6 %collective-permute-start.4 = (f32[1,3,2,512]{3,2,1,0:T(2,128)S(1)}, f32[1,3,2,512]{3,2,1,0:T(2,128)S(1)}, u32[]{:S(2)}, u32[]{:S(2)}) collective-permute-start(f32[1,3,2,512]{3,2,1,0:T(2,128)S(1)} %copy.105), channel_id=1, source_target_pairs={{0,5},{1,4},{2,7},{3,6},{4,1},{5,0},{6,3},{7,2},{8,13},{9,12},{10,... | collective-permute-start | bytes 36872 | tf_op jit(solution)/shard_map/ppermute | solution.py:134
  88.9 0.8 collective-permute-start.5
  89.8 2.7 %collective-permute-start.6 = (f32[1,3,2,512]{3,2,1,0:T(2,128)S(1)}, f32[1,3,2,512]{3,2,1,0:T(2,128)S(1)}, u32[]{:S(2)}, u32[]{:S(2)}) collective-permute-start(f32[1,3,2,512]{3,2,1,0:T(2,128)S(1)} %copy.107), channel_id=1, source_target_pairs={{0,7},{1,6},{2,5},{3,4},{4,3},{5,2},{6,1},{7,0},{8,15},{9,14},{10,... | collective-permute-start | bytes 36872 | tf_op jit(solution)/shard_map/ppermute | solution.py:134
  92.5 2.0 %collective-permute-done.5 = f32[1,3,2,512]{3,2,1,0:T(2,128)S(1)} collective-permute-done((f32[1,3,2,512]{3,2,1,0:T(2,128)S(1)}, f32[1,3,2,512]{3,2,1,0:T(2,128)S(1)}, u32[]{:S(2)}, u32[]{:S(2)}) %collective-permute-start.5) | collective-permute-done | bytes 12320 | tf_op jit(solution)/shard_map/ppermute | solution.py:134
  94.5 0.2 collective-permute-done.6
  94.7 0.6 copy-done.11
  (72 shorter events, 1.4 us)
Async XLA Ops:
  0.0 6.6 %copy-start = (f32[24,4]{0,1:T(4,128)S(1)}, f32[24,4]{0,1:T(4,128)}, u32[]{:S(2)}) copy-start(f32[24,4]{0,1:T(4,128)} %param.13) | copy-start | bytes 1156
  0.0 16.7 %copy-start.4 = (f32[32,128]{1,0:T(8,128)S(1)}, f32[32,128]{1,0:T(8,128)}, u32[]{:S(2)}) copy-start(f32[32,128]{1,0:T(8,128)} %constant.59.clone) | copy-start | bytes 49156
  0.0 16.7 %copy-start.5 = (f32[32,128]{1,0:T(8,128)S(1)}, f32[32,128]{1,0:T(8,128)}, u32[]{:S(2)}) copy-start(f32[32,128]{1,0:T(8,128)} %constant.60.clone) | copy-start | bytes 49156
  0.0 16.1 %copy-start.8 = (f32[32,128]{1,0:T(8,128)S(1)}, f32[32,128]{1,0:T(8,128)}, u32[]{:S(2)}) copy-start(f32[32,128]{1,0:T(8,128)} %constant.61.clone) | copy-start | bytes 49156
  0.0 16.1 %copy-start.9 = (f32[32,128]{1,0:T(8,128)S(1)}, f32[32,128]{1,0:T(8,128)}, u32[]{:S(2)}) copy-start(f32[32,128]{1,0:T(8,128)} %constant.63) | copy-start | bytes 49156
  0.0 16.1 %copy-start.10 = (f32[32,128]{1,0:T(8,128)S(1)}, f32[32,128]{1,0:T(8,128)}, u32[]{:S(2)}) copy-start(f32[32,128]{1,0:T(8,128)} %constant.64) | copy-start | bytes 49156
  0.0 16.4 %copy-start.1 = (f32[2,128,2,128,1]{3,1,0,2,4:T(8,128)S(1)}, f32[2,128,2,128,1]{3,1,0,2,4:T(8,128)}, u32[]{:S(2)}) copy-start(f32[2,128,2,128,1]{3,1,0,2,4:T(8,128)} %constant.67) | copy-start | bytes 786436
  0.1 16.7 %copy-start.6 = (f32[2,32,2,32,1]{1,3,0,2,4:T(8,128)S(1)}, f32[2,32,2,32,1]{1,3,0,2,4:T(8,128)}, u32[]{:S(2)}) copy-start(f32[2,32,2,32,1]{1,3,0,2,4:T(8,128)} %constant.68) | copy-start | bytes 49156
  0.1 12.8 %all-to-all-start = ((f32[8,3,2,512]{3,2,1,0:T(2,128)}), f32[8,3,2,512]{3,2,1,0:T(2,128)S(1)}, u32[]{:S(2)}, u32[]{:S(2)}) async-start(f32[8,3,2,512]{3,2,1,0:T(2,128)} %bitcast.201), calls=%async_computation | async-start | bytes 196608 | tf_op jit(solution)/shard_map/all_to_all | solution.py:108
  16.4 5.1 %copy-start.12 = (f32[96,256]{1,0:T(8,128)S(1)}, f32[96,256]{1,0:T(8,128)}, u32[]{:S(2)}) copy-start(f32[96,256]{1,0:T(8,128)} %param.12) | copy-start | bytes 294916
  18.1 14.8 %all-to-all-start.1 = ((f32[32,3,2,3,128]{4,2,1,3,0:T(2,128)}), f32[32,3,2,3,128]{4,2,1,3,0:T(2,128)S(1)}, u32[]{:S(2)}, u32[]{:S(2)}) async-start(f32[32,3,2,3,128]{4,2,1,3,0:T(2,128)} %copy.48), calls=%async_computation.1 | async-start | bytes 589824 | tf_op jit(solution)/shard_map/all_to_all | solution.py:84
  35.8 0.9 copy-start.3
  37.9 12.9 %copy-start.7 = (f32[2,32,2,32,1]{1,3,0,2,4:T(8,128)S(1)}, f32[2,32,2,32,1]{1,3,0,2,4:T(8,128)}, u32[]{:S(2)}) copy-start(f32[2,32,2,32,1]{1,3,0,2,4:T(8,128)} %constant.65) | copy-start | bytes 49156
  37.9 13.2 %copy-start.2 = (f32[2,128,2,128,1]{3,1,0,2,4:T(8,128)S(1)}, f32[2,128,2,128,1]{3,1,0,2,4:T(8,128)}, u32[]{:S(2)}) copy-start(f32[2,128,2,128,1]{3,1,0,2,4:T(8,128)} %constant.66) | copy-start | bytes 786436
  72.2 10.3 %all-to-all-start.4 = ((f32[32,3,2,128]{3,2,1,0:T(2,128)}), f32[32,3,2,128]{3,2,1,0:T(2,128)S(1)}, u32[]{:S(2)}, u32[]{:S(2)}) async-start(f32[32,3,2,128]{3,2,1,0:T(2,128)} %pad_maximum_fusion.4), calls=%async_computation.4 | async-start | bytes 196608 | tf_op jit(solution)/shard_map/all_to_all | solution.py:105
  84.1 4.8 %collective-permute-start = (f32[1,3,2,512]{3,2,1,0:T(2,128)S(1)}, f32[1,3,2,512]{3,2,1,0:T(2,128)S(1)}, u32[]{:S(2)}, u32[]{:S(2)}) collective-permute-start(f32[1,3,2,512]{3,2,1,0:T(2,128)S(1)} %copy.101), channel_id=1, source_target_pairs={{0,1},{1,0},{2,3},{3,2},{4,5},{5,4},{6,7},{7,6},{8,9},{9,8},{10,11... | collective-permute-start | bytes 36872 | tf_op jit(solution)/shard_map/ppermute | solution.py:134
  84.4 5.4 %collective-permute-start.1 = (f32[1,3,2,512]{3,2,1,0:T(2,128)S(1)}, f32[1,3,2,512]{3,2,1,0:T(2,128)S(1)}, u32[]{:S(2)}, u32[]{:S(2)}) collective-permute-start(f32[1,3,2,512]{3,2,1,0:T(2,128)S(1)} %copy.102), channel_id=1, source_target_pairs={{0,2},{1,3},{2,0},{3,1},{4,6},{5,7},{6,4},{7,5},{8,10},{9,11},{10,... | collective-permute-start | bytes 36872 | tf_op jit(solution)/shard_map/ppermute | solution.py:134
  84.8 7.7 %collective-permute-start.2 = (f32[1,3,2,512]{3,2,1,0:T(2,128)S(1)}, f32[1,3,2,512]{3,2,1,0:T(2,128)S(1)}, u32[]{:S(2)}, u32[]{:S(2)}) collective-permute-start(f32[1,3,2,512]{3,2,1,0:T(2,128)S(1)} %copy.103), channel_id=1, source_target_pairs={{0,3},{1,2},{2,1},{3,0},{4,7},{5,6},{6,5},{7,4},{8,11},{9,10},{10,... | collective-permute-start | bytes 36872 | tf_op jit(solution)/shard_map/ppermute | solution.py:134
  86.1 6.4 %collective-permute-start.3 = (f32[1,3,2,512]{3,2,1,0:T(2,128)S(1)}, f32[1,3,2,512]{3,2,1,0:T(2,128)S(1)}, u32[]{:S(2)}, u32[]{:S(2)}) collective-permute-start(f32[1,3,2,512]{3,2,1,0:T(2,128)S(1)} %copy.104), channel_id=1, source_target_pairs={{0,4},{1,5},{2,6},{3,7},{4,0},{5,1},{6,2},{7,3},{8,12},{9,13},{10,... | collective-permute-start | bytes 36872 | tf_op jit(solution)/shard_map/ppermute | solution.py:134
  86.2 6.3 %collective-permute-start.4 = (f32[1,3,2,512]{3,2,1,0:T(2,128)S(1)}, f32[1,3,2,512]{3,2,1,0:T(2,128)S(1)}, u32[]{:S(2)}, u32[]{:S(2)}) collective-permute-start(f32[1,3,2,512]{3,2,1,0:T(2,128)S(1)} %copy.105), channel_id=1, source_target_pairs={{0,5},{1,4},{2,7},{3,6},{4,1},{5,0},{6,3},{7,2},{8,13},{9,12},{10,... | collective-permute-start | bytes 36872 | tf_op jit(solution)/shard_map/ppermute | solution.py:134
  88.9 5.6 %collective-permute-start.5 = (f32[1,3,2,512]{3,2,1,0:T(2,128)S(1)}, f32[1,3,2,512]{3,2,1,0:T(2,128)S(1)}, u32[]{:S(2)}, u32[]{:S(2)}) collective-permute-start(f32[1,3,2,512]{3,2,1,0:T(2,128)S(1)} %copy.106), channel_id=1, source_target_pairs={{0,6},{1,7},{2,4},{3,5},{4,2},{5,3},{6,0},{7,1},{8,14},{9,15},{10,... | collective-permute-start | bytes 36872 | tf_op jit(solution)/shard_map/ppermute | solution.py:134
  89.8 4.9 %collective-permute-start.6 = (f32[1,3,2,512]{3,2,1,0:T(2,128)S(1)}, f32[1,3,2,512]{3,2,1,0:T(2,128)S(1)}, u32[]{:S(2)}, u32[]{:S(2)}) collective-permute-start(f32[1,3,2,512]{3,2,1,0:T(2,128)S(1)} %copy.107), channel_id=1, source_target_pairs={{0,7},{1,6},{2,5},{3,4},{4,3},{5,2},{6,1},{7,0},{8,15},{9,14},{10,... | collective-permute-start | bytes 36872 | tf_op jit(solution)/shard_map/ppermute | solution.py:134
  94.7 0.6 copy-start.11
